TPU v7x, 32 devices: a whole 2x2x4 slice. The times are simulated.
32 devices in a mesh: gx: 4 (over z), gy: 8 (over y, x, core).
Axes of the slice: x: 2, y: 2, z: 4, core: 2. Of those that a mesh axis runs over, the one named last changes fastest.
Arguments:
- source: float32 [64, 256, 512], P('gx', 'gy')
- voxel_phase: int32 [64, 256, 512], P('gx', 'gy'), may hold values from 0 to 2
- lin_potential: float32 [64, 256, 512], P('gx', 'gy'), may hold values from -1 to 1
- link_voxel: int32 [4, 8, 2048], P('gx', 'gy'), may hold values from 0 to 262143
- link_count: int32 [4, 8, 8], P('gx', 'gy'), may hold values from 1 to 256, as said below
- link_target: int32 [4, 8, 2048], P('gx', 'gy'), may hold values from 0 to 511
Outputs:
- solution: float32 [64, 256, 512], P('gx', 'gy')
- particle_current: float32 [4, 8, 512], P('gx', 'gy')
Inputs may be any that keep to these rules, and one draw needn't show every extreme that they name: `link_count`: every device has exactly 256 live links to at least one gy peer.
All inputs are finite; a program needn't handle non-finite values.
Results may differ from a plain program's by a relative error of at most 0.00012.
Values sent between devices are 32-bit elements; how exact they have to be, the bound alone decides.
A program may use at most 128 MiB of HBM per device.

v0:
```python
import jax
import jax.numpy as jnp
from jax import lax
from jax.sharding import PartitionSpec as P

ITERS = 12
PART_DEV = 512


def extended(block, sides, width):
    for axis, dim in sides:
        count = lax.axis_size(axis)
        forward = [(i, i + 1) for i in range(count - 1)]
        backward = [(target, source) for source, target in forward]
        low = lax.ppermute(
            lax.slice_in_dim(block, block.shape[dim] - width, None, axis=dim), axis, forward
        )
        high = lax.ppermute(lax.slice_in_dim(block, 0, width, axis=dim), axis, backward)
        block = jnp.concatenate([low, block, high], axis=dim)
    return block


def rate_of(voxel_phase):
    return jnp.where(voxel_phase == 1, 0.3, jnp.where(voxel_phase == 2, 0.08, 0.02)).astype(
        jnp.float32
    )


def butler(lin_potential):
    rising = jnp.exp(0.4 * lin_potential)
    falling = jnp.exp(-0.6 * lin_potential)
    return (rising - falling, 0.4 * rising + 0.6 * falling)


def operate(values, diagonal):
    padded = extended(values, (("gx", 0), ("gy", 1)), 1)
    padded = jnp.pad(padded, ((0, 0), (0, 0), (1, 1)))
    beside = padded[2:, 1:-1, 1:-1] + padded[:-2, 1:-1, 1:-1]
    beside = beside + padded[1:-1, 2:, 1:-1] + padded[1:-1, :-2, 1:-1]
    beside = beside + padded[1:-1, 1:-1, 2:] + padded[1:-1, 1:-1, :-2]
    return diagonal * values - beside


def paired_sums(residual, precond, image):
    return lax.psum((jnp.sum(residual * precond), jnp.sum(precond * image)), ("gx", "gy"))


def shards(source, voxel_phase, lin_potential, link_voxel, link_count, link_target):
    base, slope = butler(lin_potential)
    diagonal = 6.0 + rate_of(voxel_phase) * slope
    solution = jnp.zeros_like(source)
    residual = source
    precond = residual / diagonal
    image = operate(precond, diagonal)
    norm_now, product = paired_sums(residual, precond, image)
    alpha = norm_now / product
    direction, along = (precond, image)
    for iteration in range(ITERS):
        solution = solution + alpha * direction
        residual = residual - alpha * along
        if iteration + 1 < ITERS:
            precond = residual / diagonal
            image = operate(precond, diagonal)
            norm_next, product = paired_sums(residual, precond, image)
            ratio = norm_next / norm_now
            alpha = norm_next / (product - ratio * norm_next / alpha)
            direction = precond + ratio * direction
            along = image + ratio * along
            norm_now = norm_next
    current = (base + slope * solution).reshape(-1)
    peers = link_count.shape[2]
    capacity = link_voxel.shape[2] // peers
    picked = current[link_voxel[0, 0]].reshape(peers, capacity)
    within = jnp.arange(capacity)
    live = within[None, :] < link_count[0, 0][:, None]
    outgoing = jnp.where(live, 0.5 * picked, jnp.float32(0.0))
    incoming = lax.all_to_all(outgoing, "gy", split_axis=0, concat_axis=0, tiled=True)
    totals = jax.ops.segment_sum(incoming.reshape(-1), link_target[0, 0], num_segments=PART_DEV)
    return (solution, totals.reshape(1, 1, PART_DEV))


def solution(mesh):
    return jax.shard_map(
        shards,
        mesh=mesh,
        in_specs=(
            P("gx", "gy", None),
            P("gx", "gy", None),
            P("gx", "gy", None),
            P("gx", "gy", None),
            P("gx", "gy", None),
            P("gx", "gy", None),
        ),
        out_specs=(P("gx", "gy", None), P("gx", "gy", None)),
        check_vma=False,
    )
```

profile of v0, /device:TPU:0, one launch (start us, length us, event | category | flops | bytes accessed | tf_op | source)
XLA Modules:
  0.0 852.1 jit_solution(11301537836566449882)
XLA Ops:
  4.4 5.6 collective-permute-start.1
  20.7 44.0 %all-reduce.23 = (f32[]{:T(128)}, f32[]{:T(128)}) all-reduce(f32[]{:T(128)} %get-tuple-element.25, f32[]{:T(128)} %get-tuple-element.24), channel_id=1, replica_groups=mesh['gx'=4,'gy'=8] {'gx','gy'}, use_global_device_ids=true, to_apply=%region_1.2 | all-reduce | flops 2 | bytes 16 | tf_op jit(solution)/shard_map/psum | solution.py:45
  84.4 44.4 %all-reduce.22 = (f32[]{:T(128)}, f32[]{:T(128)}) all-reduce(f32[]{:T(128)} %get-tuple-element.23, f32[]{:T(128)} %get-tuple-element.22), channel_id=1, replica_groups=mesh['gx'=4,'gy'=8] {'gx','gy'}, use_global_device_ids=true, to_apply=%region_5.6 | all-reduce | flops 2 | bytes 16 | tf_op jit(solution)/shard_map/psum | solution.py:45
  137.1 4.5 collective-permute-start.9
  152.2 44.3 %all-reduce.21 = (f32[]{:T(128)}, f32[]{:T(128)}) all-reduce(f32[]{:T(128)} %get-tuple-element.21, f32[]{:T(128)} %get-tuple-element.20), channel_id=1, replica_groups=mesh['gx'=4,'gy'=8] {'gx','gy'}, use_global_device_ids=true, to_apply=%region_9.10 | all-reduce | flops 2 | bytes 16 | tf_op jit(solution)/shard_map/psum | solution.py:45
  205.8 4.5 collective-permute-start.13
  221.0 44.3 %all-reduce.20 = (f32[]{:T(128)}, f32[]{:T(128)}) all-reduce(f32[]{:T(128)} %get-tuple-element.19, f32[]{:T(128)} %get-tuple-element.18), channel_id=1, replica_groups=mesh['gx'=4,'gy'=8] {'gx','gy'}, use_global_device_ids=true, to_apply=%region_13.14 | all-reduce | flops 2 | bytes 16 | tf_op jit(solution)/shard_map/psum | solution.py:45
  273.1 4.5 collective-permute-start.17
  288.3 44.3 %all-reduce.19 = (f32[]{:T(128)}, f32[]{:T(128)}) all-reduce(f32[]{:T(128)} %get-tuple-element.17, f32[]{:T(128)} %get-tuple-element.16), channel_id=1, replica_groups=mesh['gx'=4,'gy'=8] {'gx','gy'}, use_global_device_ids=true, to_apply=%region_17.18 | all-reduce | flops 2 | bytes 16 | tf_op jit(solution)/shard_map/psum | solution.py:45
  341.5 4.5 collective-permute-start.21
  356.7 44.2 %all-reduce.18 = (f32[]{:T(128)}, f32[]{:T(128)}) all-reduce(f32[]{:T(128)} %get-tuple-element.15, f32[]{:T(128)} %get-tuple-element.14), channel_id=1, replica_groups=mesh['gx'=4,'gy'=8] {'gx','gy'}, use_global_device_ids=true, to_apply=%region_21.22 | all-reduce | flops 2 | bytes 16 | tf_op jit(solution)/shard_map/psum | solution.py:45
  423.3 44.2 %all-reduce.17 = (f32[]{:T(128)}, f32[]{:T(128)}) all-reduce(f32[]{:T(128)} %get-tuple-element.13, f32[]{:T(128)} %get-tuple-element.12), channel_id=1, replica_groups=mesh['gx'=4,'gy'=8] {'gx','gy'}, use_global_device_ids=true, to_apply=%region_25.26 | all-reduce | flops 2 | bytes 16 | tf_op jit(solution)/shard_map/psum | solution.py:45
  476.6 4.5 collective-permute-start.29
  491.7 44.3 %all-reduce.16 = (f32[]{:T(128)}, f32[]{:T(128)}) all-reduce(f32[]{:T(128)} %get-tuple-element.11, f32[]{:T(128)} %get-tuple-element.10), channel_id=1, replica_groups=mesh['gx'=4,'gy'=8] {'gx','gy'}, use_global_device_ids=true, to_apply=%region_29.30 | all-reduce | flops 2 | bytes 16 | tf_op jit(solution)/shard_map/psum | solution.py:45
  543.7 4.5 collective-permute-start.33
  558.8 44.3 %all-reduce.15 = (f32[]{:T(128)}, f32[]{:T(128)}) all-reduce(f32[]{:T(128)} %get-tuple-element.9, f32[]{:T(128)} %get-tuple-element.8), channel_id=1, replica_groups=mesh['gx'=4,'gy'=8] {'gx','gy'}, use_global_device_ids=true, to_apply=%region_33.34 | all-reduce | flops 2 | bytes 16 | tf_op jit(solution)/shard_map/psum | solution.py:45
  612.2 4.5 collective-permute-start.37
  627.4 44.3 %all-reduce.14 = (f32[]{:T(128)}, f32[]{:T(128)}) all-reduce(f32[]{:T(128)} %get-tuple-element.7, f32[]{:T(128)} %get-tuple-element.6), channel_id=1, replica_groups=mesh['gx'=4,'gy'=8] {'gx','gy'}, use_global_device_ids=true, to_apply=%region_37.38 | all-reduce | flops 2 | bytes 16 | tf_op jit(solution)/shard_map/psum | solution.py:45
  694.5 44.2 %all-reduce.13 = (f32[]{:T(128)}, f32[]{:T(128)}) all-reduce(f32[]{:T(128)} %get-tuple-element.5, f32[]{:T(128)} %get-tuple-element.4), channel_id=1, replica_groups=mesh['gx'=4,'gy'=8] {'gx','gy'}, use_global_device_ids=true, to_apply=%region_41.42 | all-reduce | flops 2 | bytes 16 | tf_op jit(solution)/shard_map/psum | solution.py:45
  760.8 44.2 %all-reduce.12 = (f32[]{:T(128)}, f32[]{:T(128)}) all-reduce(f32[]{:T(128)} %get-tuple-element.3, f32[]{:T(128)} %get-tuple-element.2), channel_id=1, replica_groups=mesh['gx'=4,'gy'=8] {'gx','gy'}, use_global_device_ids=true, to_apply=%region_45.46 | all-reduce | flops 2 | bytes 16 | tf_op jit(solution)/shard_map/psum | solution.py:45
  808.8 6.1 multiply_add_fusion
  815.2 11.8 %gather_fusion = f32[2048]{0:T(1024)S(1)} fusion(f32[262144]{0:T(1024)S(1)} %bitcast.10, s32[2048]{0:T(1024)S(1)} %broadcast_clamp_fusion), kind=kCustom, calls=%fused_computation | custom fusion | bytes 24576 | tf_op jit(solution)/shard_map/gather | solution.py:73
  827.1 9.2 %all_to_all.6 = f32[8,1,256]{2,1,0:T(1,128)S(1)} all-to-all(f32[8,1,256]{2,1,0:T(1,128)S(1)} %compare_select_fusion.1), channel_id=1, replica_groups=mesh['gx'=4,'gy'=8] {'gy'}, dimensions={0} | all-to-all | bytes 16384 | tf_op jit(solution)/shard_map/all_to_all | solution.py:77
  836.2 15.4 %scatter_custom_fusion = f32[512]{0:T(512)} fusion(s32[2048]{0:T(1024)} %bitcast.17, f32[2048]{0:T(1024)S(1)} %bitcast.14, f32[]{:T(128)} %constant.8.clone.1), kind=kCustom, calls=%fused_computation.312 | custom fusion | flops 2048 | bytes 2560 | tf_op jit(solution)/shard_map/scatter-add | solution.py:78
  (199 shorter events, 194.1 us)
Async XLA Ops:
  3.1 7.2 collective-permute-start
  4.4 7.5 collective-permute-start.1
  67.9 6.2 collective-permute-start.4
  69.2 6.4 collective-permute-start.5
  135.8 6.2 collective-permute-start.8
  137.1 6.4 collective-permute-start.9
  204.5 6.2 collective-permute-start.12
  205.8 6.4 collective-permute-start.13
  271.8 6.2 collective-permute-start.16
  273.1 6.4 collective-permute-start.17
  340.2 6.2 collective-permute-start.20
  341.5 6.4 collective-permute-start.21
  406.9 6.2 collective-permute-start.24
  408.2 6.4 collective-permute-start.25
  475.3 6.2 collective-permute-start.28
  476.6 6.4 collective-permute-start.29
  542.4 6.2 collective-permute-start.32
  543.7 6.4 collective-permute-start.33
  610.9 6.2 collective-permute-start.36
  612.2 6.4 collective-permute-start.37
  678.0 6.2 collective-permute-start.40
  679.3 6.4 collective-permute-start.41
  745.4 6.2 collective-permute-start.44
  746.7 6.4 collective-permute-start.45
  (47 other events, 403.7 us)
where the time goes:
time: 864 us; the launch traced here: 852 us
  blocking collectives  540 us (62%)
  starting transfers between devices  124 us (14%)
  other arithmetic  96.8 us (11%)
  between operations  47.2 us (5%)
  waiting for transfers between devices  32 us (4%)
  local copies, waits for them, and re-layouts  12.3 us (1%)
    psum x12, blocking collectives, paired_sums(): lax.psum((jnp.sum(residual * precond), jnp.sum(precond * image)), ('gx',...  531 us
    ppermute x24, starting transfers between devices, extended(): lax.ppermute(lax.slice_in_dim(block, block.shape[dim] - width, None, axis...  92.7 us
    div x12, other arithmetic, shards(): precond = residual / diagonal  34.3 us
    ppermute x24, starting transfers between devices, extended(): lax.ppermute(lax.slice_in_dim(block, 0, width, axis=dim), axis, backward)  31.1 us
    reduce_sum x12, other arithmetic, paired_sums(): jnp.sum(precond * image)  30 us
    ppermute x24, waiting for transfers between devices, extended(): lax.ppermute(lax.slice_in_dim(block, block.shape[dim] - width, None, axis...  28.4 us
  transfers between devices with their start and end apart: 48, of which 36 were waited for; matrix products, arithmetic and copies ran while one was open for 0% of the time, Pallas kernels for 0%

commit v1 on v0

v1 whole, which is shorter than its diff:
```python
import functools

import jax
import jax.numpy as jnp
import numpy as np
from jax import lax
from jax.experimental import pallas as pl
from jax.experimental.pallas import tpu as pltpu
from jax.sharding import PartitionSpec as P

ITERS = 12
HALF = ITERS // 2
PART_DEV = 512
ROWS = 16
RHS = 15
F32 = jnp.float32


def gram_maps():
    s = HALF

    def unit(size, at):
        out = np.zeros(size)
        out[at] = 1.0
        return out

    def own_moments(size, offset):
        moments = []
        for k in range(s):
            moments.append(2 * unit(size, offset + 2 * k + 1) - unit(size, offset + 1))
            moments.append(2 * unit(size, offset + 2 * k + 2) - unit(size, offset + 2))
        return moments

    def entry(m, j, k):
        a, b = j + k, abs(j - k)
        return 0.5 * (
            m[a] - 0.5 * (m[a + 1] + m[abs(a - 1)]) + m[b] - 0.5 * (m[b + 1] + m[abs(b - 1)])
        )

    n1 = 2 * s + 1
    first = np.zeros((n1, ROWS, 128))
    mu = own_moments(n1, 0)
    for j in range(s):
        first[:, j, RHS] = mu[j]
        for k in range(s):
            first[:, j, k] = entry(mu, j, k)
    n2 = 4 * s + 1
    size = n2 + n1
    om = own_moments(size, 0)
    mu = own_moments(size, n2)
    nu = [unit(size, n1 + m) for m in range(s)]
    nu.append(unit(size, n1 + s))
    for j in range(1, s):
        nu.append(2 * unit(size, n1 + s + j) - nu[s - j])
    second = np.zeros((size, ROWS, 128))
    for j in range(s):
        second[:, j, RHS] = nu[j]
        second[:, s + j, RHS] = om[j]
        for k in range(s):
            second[:, j, k] = entry(mu, j, k)
            second[:, s + j, s + k] = entry(om, j, k)
            second[:, j, s + k] = entry(nu, j, k)
            second[:, s + j, k] = entry(nu, j, k)
    return first.astype(np.float32), second.astype(np.float32)


def solve(matrix, count):
    rows = lax.broadcasted_iota(jnp.int32, matrix.shape, 0)
    lanes = lax.broadcasted_iota(jnp.int32, matrix.shape, 1)
    for j in range(count):
        inverse = 1.0 / matrix[j : j + 1, j : j + 1]
        factor = jnp.where(rows == j, 0.0, matrix[:, j : j + 1] * inverse)
        matrix = matrix - factor * matrix[j : j + 1, :]
    pivots = jnp.sum(jnp.where(rows == lanes, matrix, 0.0), axis=1, keepdims=True)
    answer = matrix[:, RHS : RHS + 1] / pivots
    return [jnp.broadcast_to(answer[j : j + 1, :], (8, 128)) for j in range(count)]


def kernel(
    sizes, source, phase, potential, first_map, second_map, out,
    vecs, diag, inv, xhalo, yhalo, ybuf, dots, mine, parts,
    hsend, hrecv, rsend, rrecv,
):
    n_gx, n_gy = sizes
    total = n_gx * n_gy
    cx, cy, cz = source.shape
    s = HALF
    gx, gy = lax.axis_index("gx"), lax.axis_index("gy")
    me = gx * n_gy + gy
    mesh_id = pl.DeviceIdType.MESH

    barrier = pltpu.get_barrier_semaphore()

    @pl.loop(1, total)
    def _(step):
        t = lax.rem(me + step, total)
        pl.semaphore_signal(
            barrier, inc=1, device_id=(t // n_gy, lax.rem(t, n_gy)), device_id_type=mesh_id
        )

    zero_plane = jnp.zeros((cy, cz), F32)
    dots[...] = jnp.zeros(dots.shape, F32)

    @pl.when(gy == 0)
    def _():
        yhalo[:, 0] = jnp.zeros((yhalo.shape[0],) + yhalo.shape[2:], F32)

    @pl.when(gy == n_gy - 1)
    def _():
        yhalo[:, 1] = jnp.zeros((yhalo.shape[0],) + yhalo.shape[2:], F32)

    @pl.loop(0, cx)
    def _(x):
        rising = jnp.exp(0.4 * potential[x])
        falling = jnp.exp(-0.6 * potential[x])
        label = phase[x]
        rate = jnp.where(label == 1, 0.3, jnp.where(label == 2, 0.08, 0.02)).astype(F32)
        d = 6.0 + rate * (0.4 * rising + 0.6 * falling)
        i = 1.0 / d
        diag[x] = d
        inv[x] = i
        v = source[x] * i
        vecs[0, x] = zero_plane
        vecs[s + 2, x] = zero_plane
        vecs[1, x] = v
        ybuf[1, 0, pl.ds(x, 1), :] = v[0:1, :]
        ybuf[1, 1, pl.ds(x, 1), :] = v[cy - 1 : cy, :]

    pl.semaphore_wait(barrier, total - 1)

    def copies(at):
        def make(src, dst, way, target):
            return pltpu.make_async_remote_copy(
                src_ref=src, dst_ref=dst, send_sem=hsend.at[at, way],
                recv_sem=hrecv.at[at, way], device_id=target, device_id_type=mesh_id,
            )

        up = make(vecs.at[at, cx - 1], xhalo.at[at, 0], 0, (jnp.minimum(gx + 1, n_gx - 1), gy))
        down = make(vecs.at[at, 0], xhalo.at[at, 1], 1, (jnp.maximum(gx - 1, 0), gy))
        right = make(ybuf.at[at, 1], yhalo.at[at, 0], 2, (gx, jnp.minimum(gy + 1, n_gy - 1)))
        left = make(ybuf.at[at, 0], yhalo.at[at, 1], 3, (gx, jnp.maximum(gy - 1, 0)))
        return up, down, right, left

    has_up, has_down = gx < n_gx - 1, gx > 0
    has_right, has_left = gy < n_gy - 1, gy > 0
    sends = (has_up, has_down, has_right, has_left)
    takes = (has_down, has_up, has_left, has_right)

    zlane = lax.broadcasted_iota(jnp.int32, (cy, cz), 1)
    ysub = lax.broadcasted_iota(jnp.int32, (cy, cz), 0)

    def folded(product):
        return jnp.sum(product.reshape(cy // 8, 8, cz), axis=0)

    def chain_step(base, k, second):
        now = base + 1 + k
        scale = jnp.where(k == 0, 1.0, 2.0).astype(F32)
        moves = copies(now)
        for move, there in zip(moves, sends):
            pl.when(there)(move.start)

        def plane(x, carry, low, high):
            c = vecs[now, x]
            before = vecs[now - 1, x]
            n = jnp.where(zlane == 0, 0.0, pltpu.roll(c, 1, 1))
            n = n + jnp.where(zlane == cz - 1, 0.0, pltpu.roll(c, cz - 1, 1))
            n = n + jnp.where(ysub == 0, 0.0, pltpu.roll(c, 1, 0))
            n = n + jnp.where(ysub == cy - 1, 0.0, pltpu.roll(c, cy - 1, 0))
            if low:
                n = n + vecs[now, x - 1]
            if high:
                n = n + vecs[now, x + 1]
            vecs[now + 1, x] = (scale * inv[x]) * n - before
            weighted = diag[x] * c
            found = [weighted * c, weighted * before]
            if second:
                found.append(weighted * vecs[s + 1, x])
                found.append(diag[x] * vecs[s + 3, x] * vecs[1 + k, x])
            return tuple(a + folded(b) for a, b in zip(carry, found))

        carry = tuple(jnp.zeros((8, cz), F32) for _ in range(4 if second else 2))
        carry = plane(0, carry, False, True)
        carry = lax.fori_loop(1, cx - 1, lambda x, a: plane(x, a, True, True), carry)
        carry = plane(cx - 1, carry, True, False)
        dots[2 * k + 1] = carry[0]
        dots[2 * k] = carry[1]
        if second:
            dots[3 * s + 1 + k] = carry[2]
            dots[2 * s + 1 + k] = carry[3]

        for way in (2, 3):
            pl.when(takes[way])(moves[way].wait_recv)

        @pl.when(takes[0])
        def _():
            moves[0].wait_recv()
            vecs[now + 1, 0] = vecs[now + 1, 0] + (scale * inv[0]) * xhalo[now, 0]

        @pl.when(takes[1])
        def _():
            moves[1].wait_recv()
            vecs[now + 1, cx - 1] = (
                vecs[now + 1, cx - 1] + (scale * inv[cx - 1]) * xhalo[now, 1]
            )

        for x in range(cx):
            for side, y in ((0, 0), (1, cy - 1)):
                row = vecs[now + 1, x, y : y + 1, :] + (
                    scale * inv[x, y : y + 1, :]
                ) * yhalo[now, side, x : x + 1, :]
                vecs[now + 1, x, y : y + 1, :] = row
                ybuf[now + 1, side, x : x + 1, :] = row
        for move, there in zip(moves, sends):
            pl.when(there)(move.wait_send)

    def run_chain(base, second):
        @pl.loop(0, s)
        def _(k):
            chain_step(base, k, second)

        def last(x, a):
            return a + folded(diag[x] * vecs[base + s, x] * vecs[base + s + 1, x])

        dots[2 * s] = lax.fori_loop(0, cx, last, jnp.zeros((8, cz), F32))

    def reduced(which):
        part = jnp.sum(dots[...], axis=1)
        part = sum(part[:, 128 * z : 128 * (z + 1)] for z in range(cz // 128))
        part = jnp.sum(part, axis=1, keepdims=True)
        rows = lax.broadcasted_iota(jnp.int32, (dots.shape[0], 128), 0)
        lanes = lax.broadcasted_iota(jnp.int32, (dots.shape[0], 128), 1)
        row = jnp.sum(jnp.where(rows == lanes, part, 0.0), axis=0, keepdims=True)
        mine[which] = row
        parts[which, me] = row

        def move(owner, target):
            return pltpu.make_async_remote_copy(
                src_ref=mine.at[which], dst_ref=parts.at[which, owner],
                send_sem=rsend.at[which, target], recv_sem=rrecv.at[which, owner],
                device_id=(target // n_gy, lax.rem(target, n_gy)), device_id_type=mesh_id,
            )

        @pl.loop(1, total)
        def _(step):
            move(me, lax.rem(me + step, total)).start()

        @pl.loop(1, total)
        def _(step):
            other = lax.rem(me + step, total)
            move(other, other).wait_recv()

        @pl.loop(1, total)
        def _(step):
            move(me, lax.rem(me + step, total)).wait_send()

        return jnp.sum(parts[which], axis=0)

    def assembled(table, values):
        return sum(
            table[m] * jnp.broadcast_to(values[m][0][:, values[m][1] : values[m][1] + 1], (ROWS, 128))
            for m in range(table.shape[0])
        )

    def combine(coefficients, slots, store):
        @pl.loop(0, cx)
        def _(x):
            for y in range(0, cy, 8):
                for z in range(0, cz, 128):
                    pieces = [
                        w * vecs[slot, x, y : y + 8, z : z + 128]
                        for w, slot in zip(coefficients, slots)
                    ]
                    while len(pieces) > 1:
                        pieces = [sum(pieces[i : i + 2]) for i in range(0, len(pieces), 2)]
                    store(x, y, z, pieces[0])

    run_chain(0, False)
    sums = reduced(0)
    n1, n2 = 2 * s + 1, 4 * s + 1
    first = solve(assembled(first_map, [(sums, m) for m in range(n1)]), s)
    tail = [jnp.ones((8, 128), F32)] + [jnp.zeros((8, 128), F32) for _ in range(s)]
    for k in range(s):
        tail[k] = tail[k] - first[k]
        tail[k + 1] = tail[k + 1] + 0.5 * first[k]
        tail[abs(k - 1)] = tail[abs(k - 1)] + 0.5 * first[k]
    base = s + 2

    def keep(x, y, z, value):
        vecs[base + 1, x, y : y + 8, z : z + 128] = value

    combine(tail, range(1, s + 2), keep)
    for x in range(cx):
        ybuf[base + 1, 0, x : x + 1, :] = vecs[base + 1, x, 0:1, :]
        ybuf[base + 1, 1, x : x + 1, :] = vecs[base + 1, x, cy - 1 : cy, :]
    run_chain(base, True)
    again = reduced(1)
    values = [(again, m) for m in range(n2)] + [(sums, m) for m in range(n1)]
    second = solve(assembled(second_map, values), 2 * s)
    weights = [first[k] + second[k] for k in range(s)] + second[s:]

    def emit(x, y, z, value):
        out[x, y : y + 8, z : z + 128] = value

    combine(weights, list(range(1, s + 1)) + list(range(base + 1, base + s + 1)), emit)


def solved(sizes, source, voxel_phase, lin_potential):
    cx, cy, cz = source.shape
    total = sizes[0] * sizes[1]
    slots = 2 * HALF + 4
    first_map, second_map = gram_maps()
    lanes = 4 * HALF + 8
    whole = pl.BlockSpec(memory_space=pltpu.VMEM)
    return pl.pallas_call(
        functools.partial(kernel, sizes),
        out_shape=jax.ShapeDtypeStruct(source.shape, F32),
        in_specs=[whole] * 5,
        out_specs=whole,
        scratch_shapes=[
            pltpu.VMEM((slots, cx, cy, cz), F32),
            pltpu.VMEM((cx, cy, cz), F32),
            pltpu.VMEM((cx, cy, cz), F32),
            pltpu.VMEM((slots, 2, cy, cz), F32),
            pltpu.VMEM((slots, 2, cx, cz), F32),
            pltpu.VMEM((slots, 2, cx, cz), F32),
            pltpu.VMEM((lanes, 8, cz), F32),
            pltpu.VMEM((2, 1, 128), F32),
            pltpu.VMEM((2, total, 1, 128), F32),
            pltpu.SemaphoreType.DMA((slots, 4)),
            pltpu.SemaphoreType.DMA((slots, 4)),
            pltpu.SemaphoreType.DMA((2, total)),
            pltpu.SemaphoreType.DMA((2, total)),
        ],
        compiler_params=pltpu.CompilerParams(collective_id=0, has_side_effects=True),
    )(source, voxel_phase, lin_potential, jnp.asarray(first_map), jnp.asarray(second_map))


def butler(lin_potential):
    rising = jnp.exp(0.4 * lin_potential)
    falling = jnp.exp(-0.6 * lin_potential)
    return (rising - falling, 0.4 * rising + 0.6 * falling)


def shards(sizes, source, voxel_phase, lin_potential, link_voxel, link_count, link_target):
    solution = solved(sizes, source, voxel_phase, lin_potential)
    at = link_voxel[0, 0]
    base, slope = butler(lin_potential.reshape(-1)[at])
    current = base + slope * solution.reshape(-1)[at]
    peers = link_count.shape[2]
    capacity = link_voxel.shape[2] // peers
    picked = current.reshape(peers, capacity)
    within = jnp.arange(capacity)
    live = within[None, :] < link_count[0, 0][:, None]
    outgoing = jnp.where(live, 0.5 * picked, jnp.float32(0.0))
    incoming = lax.all_to_all(outgoing, "gy", split_axis=0, concat_axis=0, tiled=True)
    totals = jax.ops.segment_sum(incoming.reshape(-1), link_target[0, 0], num_segments=PART_DEV)
    return (solution, totals.reshape(1, 1, PART_DEV))


def solution(mesh):
    spec = P("gx", "gy", None)
    return jax.shard_map(
        functools.partial(shards, (mesh.shape["gx"], mesh.shape["gy"])),
        mesh=mesh,
        in_specs=(spec,) * 6,
        out_specs=(spec, spec),
        check_vma=False,
    )
```

time: 864 us -> 118 us (0.14); the launches traced: 852 us -> 118 us
  blocking collectives: 540 us -> 7.06 us
  starting transfers between devices: 124 us -> 0 us
  other arithmetic: 96.8 us -> 16.2 us
  Pallas kernels: 0 us -> 67.1 us
  between operations: 47.2 us -> 0.71 us
  waiting for transfers between devices: 32 us -> 0 us
  local copies, waits for them, and re-layouts: 12.3 us -> 27.1 us
    psum x12 -> x0, blocking collectives: 531 us -> none  [paired_sums(): lax.psum((jnp.sum(residual * precond), jnp.sum(precond * image)), ('gx',...]
    ppermute x48 -> x0, starting transfers between devices: 124 us -> none  [the longest x24 92.7 us: extended(): lax.ppermute(lax.slice_in_dim(block, block.shape[dim] - width, None, axis...]
    pallas_call x0 -> x1, Pallas kernels: none -> 67.1 us  [solved(): pl.pallas_call(functools.partial(kernel, sizes), out_shape=jax.ShapeDtype...]
    div x12 -> x0, other arithmetic: 34.3 us -> none  [shards(): precond = residual / diagonal]
    ppermute x48 -> x0, waiting for transfers between devices: 32 us -> none  [the longest x24 28.4 us: extended(): lax.ppermute(lax.slice_in_dim(block, block.shape[dim] - width, None, axis...]
    reduce_sum x12 -> x0, other arithmetic: 30 us -> none  [paired_sums(): jnp.sum(precond * image)]
    gather x1 -> x2, local copies, waits for them, and re-layouts: 11.8 us -> 23.6 us  [the longest x1 11.8 us: shards(): current = base + slope * solution.reshape(-1)[at]]
    concatenate x24 -> x0, other arithmetic: 10.8 us -> none  [extended(): block = jnp.concatenate([low, block, high], axis=dim)]
  transfers between devices with their start and end apart: 48 -> 0, of which waited for: 36 -> 0; matrix products, arithmetic and copies ran while one was open for 0% -> 0% of each run, Pallas kernels for 0% -> 0%
where the time goes in v1:
time: 118 us
  Pallas kernels  67.1 us (57%)
  local copies, waits for them, and re-layouts  27.1 us (23%)
  other arithmetic  16.2 us (14%)
  blocking collectives  7.06 us (6%)
    pallas_call x1, Pallas kernels, solved(): pl.pallas_call(functools.partial(kernel, sizes), out_shape=jax.ShapeDtype...  67.1 us
    scatter-add x1, other arithmetic, shards(): jax.ops.segment_sum(incoming.reshape(-1), link_target[0, 0], num_segments...  15.4 us
    gather x1, local copies, waits for them, and re-layouts, shards(): current = base + slope * solution.reshape(-1)[at]  11.8 us
    gather x1, local copies, waits for them, and re-layouts, shards(): base, slope = butler(lin_potential.reshape(-1)[at])  11.8 us
    all_to_all x1, blocking collectives, shards(): lax.all_to_all(outgoing, 'gy', split_axis=0, concat_axis=0, tiled=True)  7.06 us
    unnamed x9, local copies, waits for them, and re-layouts  3.49 us

profile of v1, /device:TPU:0, one launch (start us, length us, event | category | flops | bytes accessed | tf_op | source)
XLA Modules:
  0.0 118.1 jit_solution(11495952432143609032)
XLA Ops:
  0.6 0.7 compare_select_fusion
  1.4 67.1 %shard_map.95 = f32[16,32,512]{2,1,0:T(8,128)} custom-call(f32[16,32,512]{2,1,0:T(8,128)} %source.1, s32[16,32,512]{2,1,0:T(8,128)} %phase.1, f32[16,32,512]{2,1,0:T(8,128)} %potential.1, f32[13,16,128]{2,1,0:T(8,128)} %constant.8.clone.first_map, f32[38,16,128]{2,1,0:T(8,128)} %constant.20.clone.second_map), custom_call_target="tpu_custom_call" | custom-call | tf_op jit(solution)/shard_map/pallas_call | solution.py:314
  68.5 0.0 copy-start.1
  68.5 1.6 %copy.11 = f32[64,4,8,128]{3,1,2,0:T(4,128)S(1)} copy(f32[64,4,8,128]{3,2,1,0:T(8,128)} %bitcast.14) | data formatting | bytes 2097152
  70.1 0.0 copy-done.1
  70.1 0.3 copy.10
  70.4 11.8 %gather_fusion.1 = f32[2048]{0:T(1024)S(1)} fusion(f32[262144]{0:T(1024)S(1)} %bitcast.13, s32[2048]{0:T(1024)S(1)} %broadcast_clamp_fusion), kind=kCustom, calls=%fused_computation.1 | custom fusion | bytes 24576 | tf_op jit(solution)/shard_map/gather | solution.py:348
  82.2 0.0 copy-start
  82.2 11.8 %gather_fusion = f32[2048]{0:T(1024)S(1)} fusion(f32[262144]{0:T(1024)S(1)} %bitcast.12, s32[2048]{0:T(1024)S(1)} %broadcast_clamp_fusion), kind=kCustom, calls=%fused_computation | custom fusion | bytes 24576 | tf_op jit(solution)/shard_map/gather | solution.py:347
  94.0 0.0 copy-start.2
  94.0 0.6 copy-done.2
  94.6 0.1 compare_select_fusion.1
  94.7 7.1 %all_to_all.6 = f32[8,1,256]{2,1,0:T(1,128)S(1)} all-to-all(f32[8,1,256]{2,1,0:T(1,128)S(1)} %compare_select_fusion.1), channel_id=1, replica_groups=mesh['gx'=4,'gy'=8] {'gy'}, dimensions={0} | all-to-all | bytes 16384 | tf_op jit(solution)/shard_map/all_to_all | solution.py:355
  101.8 15.4 %scatter_custom_fusion = f32[512]{0:T(512)} fusion(s32[2048]{0:T(1024)} %bitcast.21, f32[2048]{0:T(1024)S(1)} %bitcast.18, f32[]{:T(128)} %constant.9.clone.1), kind=kCustom, calls=%fused_computation.7 | custom fusion | flops 2048 | bytes 2560 | tf_op jit(solution)/shard_map/scatter-add | solution.py:356
  117.2 0.0 copy-done
  117.2 1.0 copy.13
  (2 shorter events, 0.0 us)
Async XLA Ops:
  68.5 1.6 %copy-start.1 = (f32[16,32,512]{2,1,0:T(8,128)S(1)}, f32[16,32,512]{2,1,0:T(8,128)}, u32[]{:S(2)}) copy-start(f32[16,32,512]{2,1,0:T(8,128)} %potential.1) | copy-start | bytes 3145732
  82.2 35.0 %copy-start = (f32[16,32,512]{2,1,0:T(8,128)S(1)}, f32[16,32,512]{2,1,0:T(8,128)}, u32[]{:S(2)}) copy-start(f32[16,32,512]{2,1,0:T(8,128)} %shard_map.95) | copy-start | bytes 3145732
  94.0 0.7 copy-start.2

commit v2 on v1

--- a/solution.py
+++ b/solution.py
@@ -77,9 +77,9 @@
 
 
 def kernel(
-    sizes, source, phase, potential, first_map, second_map, out,
-    vecs, diag, inv, xhalo, yhalo, ybuf, dots, mine, parts,
-    hsend, hrecv, rsend, rrecv,
+    sizes, source, phase, potential, first_map, second_map, voxel, count, target, out, particle,
+    vecs, diag, inv, xhalo, yhalo, ybuf, dots, mine, parts, pick, level, sent, got,
+    hsend, hrecv, rsend, rrecv, lsend, lrecv,
 ):
     n_gx, n_gy = sizes
     total = n_gx * n_gy
@@ -223,7 +223,31 @@
 
         dots[2 * s] = lax.fori_loop(0, cx, last, jnp.zeros((8, cz), F32))
 
-    def reduced(which):
+    groups = target.shape[0]
+    wide = groups // n_gy
+    lane = lax.broadcasted_iota(jnp.int32, (1, 128), 1)
+    zbits, ybits = cz.bit_length() - 1, cy.bit_length() - 1
+
+    def gathered(ref, group):
+        @pl.loop(0, 128, step=16)
+        def _(start):
+            for i in range(16):
+                v = voxel[group * 128 + start + i]
+                row = ref[v >> (zbits + ybits), pl.ds((v >> zbits) & (cy - 1), 1), :]
+                spot = v & (cz - 1)
+                kept = jnp.zeros((1, 128), F32)
+                for z in range(0, cz, 128):
+                    kept = jnp.where(lane == spot - z, row[:, z : z + 128], kept)
+                pick[pl.ds(start + i, 1), :] = kept
+
+        return jnp.sum(pick[...].T, axis=0, keepdims=True)
+
+    def levels(start, stop):
+        @pl.loop(start, stop)
+        def _(group):
+            level[pl.ds(group, 1), :] = gathered(potential, group)
+
+    def reduced(which, meanwhile):
         part = jnp.sum(dots[...], axis=1)
         part = sum(part[:, 128 * z : 128 * (z + 1)] for z in range(cz // 128))
         part = jnp.sum(part, axis=1, keepdims=True)
@@ -243,6 +267,8 @@
         @pl.loop(1, total)
         def _(step):
             move(me, lax.rem(me + step, total)).start()
+
+        meanwhile()
 
         @pl.loop(1, total)
         def _(step):
@@ -275,7 +301,7 @@
                     store(x, y, z, pieces[0])
 
     run_chain(0, False)
-    sums = reduced(0)
+    sums = reduced(0, lambda: levels(0, groups // 2))
     n1, n2 = 2 * s + 1, 4 * s + 1
     first = solve(assembled(first_map, [(sums, m) for m in range(n1)]), s)
     tail = [jnp.ones((8, 128), F32)] + [jnp.zeros((8, 128), F32) for _ in range(s)]
@@ -293,7 +319,7 @@
         ybuf[base + 1, 0, x : x + 1, :] = vecs[base + 1, x, 0:1, :]
         ybuf[base + 1, 1, x : x + 1, :] = vecs[base + 1, x, cy - 1 : cy, :]
     run_chain(base, True)
-    again = reduced(1)
+    again = reduced(1, lambda: levels(groups // 2, groups))
     values = [(again, m) for m in range(n2)] + [(sums, m) for m in range(n1)]
     second = solve(assembled(second_map, values), 2 * s)
     weights = [first[k] + second[k] for k in range(s)] + second[s:]
@@ -303,19 +329,72 @@
 
     combine(weights, list(range(1, s + 1)) + list(range(base + 1, base + s + 1)), emit)
 
-
-def solved(sizes, source, voxel_phase, lin_potential):
+    @pl.loop(0, n_gy)
+    def _(peer):
+        live = count[peer]
+        for part in range(wide):
+            group = peer * wide + part
+            at = level[pl.ds(group, 1), :]
+            rising = jnp.exp(0.4 * at)
+            falling = jnp.exp(-0.6 * at)
+            slope = 0.4 * rising + 0.6 * falling
+            current = (rising - falling) + slope * gathered(out, group)
+            sent[peer, part : part + 1, :] = jnp.where(
+                lane + 128 * part < live, 0.5 * current, 0.0
+            )
+
+    def link(owner, peer):
+        return pltpu.make_async_remote_copy(
+            src_ref=sent.at[peer], dst_ref=got.at[owner], send_sem=lsend.at[peer],
+            recv_sem=lrecv.at[owner], device_id=(gx, peer), device_id_type=mesh_id,
+        )
+
+    @pl.loop(1, n_gy)
+    def _(step):
+        link(gy, lax.rem(gy + step, n_gy)).start()
+
+    got[gy] = sent[gy]
+
+    @pl.loop(1, n_gy)
+    def _(step):
+        other = lax.rem(gy + step, n_gy)
+        link(other, other).wait_recv()
+
+    own = particle.shape[1]
+    sub = lax.broadcasted_iota(jnp.int32, (128, 128), 0)
+    for start in range(0, own, 128):
+        def add(peer, acc):
+            for part in range(wide):
+                spot = target[pl.ds(peer * wide + part, 1), :]
+                acc = acc + jnp.where(spot - start == sub, got[peer, part : part + 1, :], 0.0)
+            return acc
+
+        acc = lax.fori_loop(0, n_gy, add, jnp.zeros((128, 128), F32))
+        particle[:, start : start + 128] = jnp.sum(acc.T, axis=0, keepdims=True)
+
+    @pl.loop(1, n_gy)
+    def _(step):
+        link(gy, lax.rem(gy + step, n_gy)).wait_send()
+
+
+def shards(sizes, source, voxel_phase, lin_potential, link_voxel, link_count, link_target):
     cx, cy, cz = source.shape
     total = sizes[0] * sizes[1]
     slots = 2 * HALF + 4
     first_map, second_map = gram_maps()
     lanes = 4 * HALF + 8
     whole = pl.BlockSpec(memory_space=pltpu.VMEM)
-    return pl.pallas_call(
+    peers = link_count.shape[2]
+    groups = link_voxel.shape[2] // 128
+    scalars = pl.BlockSpec(memory_space=pltpu.SMEM)
+    values, totals = pl.pallas_call(
         functools.partial(kernel, sizes),
-        out_shape=jax.ShapeDtypeStruct(source.shape, F32),
-        in_specs=[whole] * 5,
-        out_specs=whole,
+        out_shape=(
+            jax.ShapeDtypeStruct(source.shape, F32),
+            jax.ShapeDtypeStruct((1, PART_DEV), F32),
+        ),
+        in_specs=[whole] * 5 + [scalars, scalars, whole],
+        out_specs=(whole, whole),
         scratch_shapes=[
             pltpu.VMEM((slots, cx, cy, cz), F32),
             pltpu.VMEM((cx, cy, cz), F32),
@@ -326,35 +405,23 @@
             pltpu.VMEM((lanes, 8, cz), F32),
             pltpu.VMEM((2, 1, 128), F32),
             pltpu.VMEM((2, total, 1, 128), F32),
+            pltpu.VMEM((128, 128), F32),
+            pltpu.VMEM((groups, 128), F32),
+            pltpu.VMEM((peers, groups // peers, 128), F32),
+            pltpu.VMEM((peers, groups // peers, 128), F32),
             pltpu.SemaphoreType.DMA((slots, 4)),
             pltpu.SemaphoreType.DMA((slots, 4)),
             pltpu.SemaphoreType.DMA((2, total)),
             pltpu.SemaphoreType.DMA((2, total)),
+            pltpu.SemaphoreType.DMA((peers,)),
+            pltpu.SemaphoreType.DMA((peers,)),
         ],
         compiler_params=pltpu.CompilerParams(collective_id=0, has_side_effects=True),
-    )(source, voxel_phase, lin_potential, jnp.asarray(first_map), jnp.asarray(second_map))
-
-
-def butler(lin_potential):
-    rising = jnp.exp(0.4 * lin_potential)
-    falling = jnp.exp(-0.6 * lin_potential)
-    return (rising - falling, 0.4 * rising + 0.6 * falling)
-
-
-def shards(sizes, source, voxel_phase, lin_potential, link_voxel, link_count, link_target):
-    solution = solved(sizes, source, voxel_phase, lin_potential)
-    at = link_voxel[0, 0]
-    base, slope = butler(lin_potential.reshape(-1)[at])
-    current = base + slope * solution.reshape(-1)[at]
-    peers = link_count.shape[2]
-    capacity = link_voxel.shape[2] // peers
-    picked = current.reshape(peers, capacity)
-    within = jnp.arange(capacity)
-    live = within[None, :] < link_count[0, 0][:, None]
-    outgoing = jnp.where(live, 0.5 * picked, jnp.float32(0.0))
-    incoming = lax.all_to_all(outgoing, "gy", split_axis=0, concat_axis=0, tiled=True)
-    totals = jax.ops.segment_sum(incoming.reshape(-1), link_target[0, 0], num_segments=PART_DEV)
-    return (solution, totals.reshape(1, 1, PART_DEV))
+    )(
+        source, voxel_phase, lin_potential, jnp.asarray(first_map), jnp.asarray(second_map),
+        link_voxel[0, 0], link_count[0, 0], link_target[0, 0].reshape(groups, 128),
+    )
+    return values, totals.reshape(1, 1, PART_DEV)
 
 
 def solution(mesh):

time: 118 us -> 90.4 us (0.77)
  local copies, waits for them, and re-layouts: 27.1 us -> 2.87 us
  Pallas kernels: 67.1 us -> 86.7 us
  other arithmetic: 16.2 us -> 0 us
  blocking collectives: 7.06 us -> 0 us
    gather x2 -> x0, local copies, waits for them, and re-layouts: 23.6 us -> none  [the longest x1 11.8 us: shards(): current = base + slope * solution.reshape(-1)[at]]
    pallas_call x1, Pallas kernels: 67.1 us -> 86.7 us  [shards(): pl.pallas_call(functools.partial(kernel, sizes), out_shape=(jax.ShapeDtyp...]
    scatter-add x1 -> x0, other arithmetic: 15.4 us -> none  [shards(): jax.ops.segment_sum(incoming.reshape(-1), link_target[0, 0], num_segments...]
    all_to_all x1 -> x0, blocking collectives: 7.06 us -> none  [shards(): lax.all_to_all(outgoing, 'gy', split_axis=0, concat_axis=0, tiled=True)]
    unnamed x9 -> x4, local copies, waits for them, and re-layouts: 3.49 us -> 2.87 us
where the time goes in v2:
time: 90.4 us; the launch traced here: 90.2 us
  Pallas kernels  86.7 us (96%)
  local copies, waits for them, and re-layouts  2.87 us (3%)
    pallas_call x1, Pallas kernels, shards(): pl.pallas_call(functools.partial(kernel, sizes), out_shape=(jax.ShapeDtyp...  86.7 us
    unnamed x4, local copies, waits for them, and re-layouts  2.87 us

profile of v2, /device:TPU:0, one launch (start us, length us, event | category | flops | bytes accessed | tf_op | source)
XLA Modules:
  0.0 90.2 jit_solution(13382865401073105853)
XLA Ops:
  0.6 86.7 %shard_map.95 = (f32[16,32,512]{2,1,0:T(8,128)}, f32[1,512]{1,0:T(1,128)}) custom-call(f32[16,32,512]{2,1,0:T(8,128)} %source.1, s32[16,32,512]{2,1,0:T(8,128)} %phase.1, f32[16,32,512]{2,1,0:T(8,128)} %potential.1, f32[13,16,128]{2,1,0:T(8,128)} %constant.4.clone.first_map, f32[38,16,128]{2,1,0:T(8,128)} %constant.5.clone.second_map, s32[2048]{0:T(1024)} %bitcast.4, ...), custom_call_target="tpu_custom_call" | custom-call | tf_op jit(solution)/shard_map/pallas_call | solution.py:390
  87.3 0.0 copy-start
  87.3 2.3 %copy.12 = f32[16,32,512]{2,1,0:T(8,128)} copy(f32[16,32,512]{2,1,0:T(8,128)} %get-tuple-element.8) | data formatting | bytes 2097152
  89.6 0.0 copy-done
  89.6 0.6 copy.13
Async XLA Ops:
  87.3 2.3 %copy-start = (f32[1,512]{1,0:T(1,128)S(1)}, f32[1,512]{1,0:T(1,128)}, u32[]{:S(2)}) copy-start(f32[1,512]{1,0:T(1,128)} %get-tuple-element.5) | copy-start | bytes 6148

commit v3 on v2

--- a/solution.py
+++ b/solution.py
@@ -78,7 +78,7 @@
 
 def kernel(
     sizes, source, phase, potential, first_map, second_map, voxel, count, target, out, particle,
-    vecs, diag, inv, xhalo, yhalo, ybuf, dots, mine, parts, pick, level, sent, got,
+    vecs, diag, inv, xhalo, yhalo, ybuf, dots, mine, parts, pick, flat, level, sent, got,
     hsend, hrecv, rsend, rrecv, lsend, lrecv,
 ):
     n_gx, n_gy = sizes
@@ -125,8 +125,6 @@
         vecs[1, x] = v
         ybuf[1, 0, pl.ds(x, 1), :] = v[0:1, :]
         ybuf[1, 1, pl.ds(x, 1), :] = v[cy - 1 : cy, :]
-
-    pl.semaphore_wait(barrier, total - 1)
 
     def copies(at):
         def make(src, dst, way, target):
@@ -225,27 +223,27 @@
 
     groups = target.shape[0]
     wide = groups // n_gy
+    tiles = cz // 128
     lane = lax.broadcasted_iota(jnp.int32, (1, 128), 1)
-    zbits, ybits = cz.bit_length() - 1, cy.bit_length() - 1
 
     def gathered(ref, group):
-        @pl.loop(0, 128, step=16)
+        @pl.loop(0, 128, step=32)
         def _(start):
-            for i in range(16):
+            for i in range(32):
                 v = voxel[group * 128 + start + i]
-                row = ref[v >> (zbits + ybits), pl.ds((v >> zbits) & (cy - 1), 1), :]
-                spot = v & (cz - 1)
-                kept = jnp.zeros((1, 128), F32)
-                for z in range(0, cz, 128):
-                    kept = jnp.where(lane == spot - z, row[:, z : z + 128], kept)
-                pick[pl.ds(start + i, 1), :] = kept
+                row = ref[pl.ds(v >> 7, 1), :]
+                pick[pl.ds(start + i, 1), :] = jnp.where(lane == (v & 127), row, 0.0)
 
         return jnp.sum(pick[...].T, axis=0, keepdims=True)
+
+    def flatten(x, y, z, value):
+        start = (x * cy + y) * tiles + z // 128
+        flat[pl.ds(start, 8, stride=tiles), :] = value
 
     def levels(start, stop):
         @pl.loop(start, stop)
         def _(group):
-            level[pl.ds(group, 1), :] = gathered(potential, group)
+            level[pl.ds(group, 1), :] = gathered(flat, group)
 
     def reduced(which, meanwhile):
         part = jnp.sum(dots[...], axis=1)
@@ -300,6 +298,13 @@
                         pieces = [sum(pieces[i : i + 2]) for i in range(0, len(pieces), 2)]
                     store(x, y, z, pieces[0])
 
+    @pl.loop(0, cx)
+    def _(x):
+        for y in range(0, cy, 8):
+            for z in range(0, cz, 128):
+                flatten(x, y, z, potential[x, y : y + 8, z : z + 128])
+
+    pl.semaphore_wait(barrier, total - 1)
     run_chain(0, False)
     sums = reduced(0, lambda: levels(0, groups // 2))
     n1, n2 = 2 * s + 1, 4 * s + 1
@@ -326,6 +331,7 @@
 
     def emit(x, y, z, value):
         out[x, y : y + 8, z : z + 128] = value
+        flatten(x, y, z, value)
 
     combine(weights, list(range(1, s + 1)) + list(range(base + 1, base + s + 1)), emit)
 
@@ -338,7 +344,7 @@
             rising = jnp.exp(0.4 * at)
             falling = jnp.exp(-0.6 * at)
             slope = 0.4 * rising + 0.6 * falling
-            current = (rising - falling) + slope * gathered(out, group)
+            current = (rising - falling) + slope * gathered(flat, group)
             sent[peer, part : part + 1, :] = jnp.where(
                 lane + 128 * part < live, 0.5 * current, 0.0
             )
@@ -406,6 +412,7 @@
             pltpu.VMEM((2, 1, 128), F32),
             pltpu.VMEM((2, total, 1, 128), F32),
             pltpu.VMEM((128, 128), F32),
+            pltpu.VMEM((cx * cy * (cz // 128), 128), F32),
             pltpu.VMEM((groups, 128), F32),
             pltpu.VMEM((peers, groups // peers, 128), F32),
             pltpu.VMEM((peers, groups // peers, 128), F32),

time: 90.4 us -> 79.3 us (0.88)
  Pallas kernels: 86.7 us -> 75.7 us
    pallas_call x1, Pallas kernels: 86.7 us -> 75.7 us  [shards(): pl.pallas_call(functools.partial(kernel, sizes), out_shape=(jax.ShapeDtyp...]
where the time goes in v3:
time: 79.3 us; the launch traced here: 79.2 us
  Pallas kernels  75.7 us (95%)
  local copies, waits for them, and re-layouts  2.87 us (4%)
    pallas_call x1, Pallas kernels, shards(): pl.pallas_call(functools.partial(kernel, sizes), out_shape=(jax.ShapeDtyp...  75.7 us
    unnamed x4, local copies, waits for them, and re-layouts  2.87 us

profile of v3, /device:TPU:0, one launch (start us, length us, event | category | flops | bytes accessed | tf_op | source)
XLA Modules:
  0.0 79.2 jit_solution(9280883410084772041)
XLA Ops:
  0.6 75.7 %shard_map.95 = (f32[16,32,512]{2,1,0:T(8,128)}, f32[1,512]{1,0:T(1,128)}) custom-call(f32[16,32,512]{2,1,0:T(8,128)} %source.1, s32[16,32,512]{2,1,0:T(8,128)} %phase.1, f32[16,32,512]{2,1,0:T(8,128)} %potential.1, f32[13,16,128]{2,1,0:T(8,128)} %constant.4.clone.first_map, f32[38,16,128]{2,1,0:T(8,128)} %constant.5.clone.second_map, s32[2048]{0:T(1024)} %bitcast.4, ...), custom_call_target="tpu_custom_call" | custom-call | tf_op jit(solution)/shard_map/pallas_call | solution.py:396
  76.3 0.0 copy-start
  76.3 2.3 %copy.12 = f32[16,32,512]{2,1,0:T(8,128)} copy(f32[16,32,512]{2,1,0:T(8,128)} %get-tuple-element.8) | data formatting | bytes 2097152
  78.6 0.0 copy-done
  78.6 0.6 copy.13
Async XLA Ops:
  76.3 2.3 %copy-start = (f32[1,512]{1,0:T(1,128)S(1)}, f32[1,512]{1,0:T(1,128)}, u32[]{:S(2)}) copy-start(f32[1,512]{1,0:T(1,128)} %get-tuple-element.5) | copy-start | bytes 6148
